TPU v7x, 32 devices: a whole 2x2x4 slice. The times are simulated.
32 devices in a mesh: ctx: 8 (over z, x), tp: 4 (over y, core).
Axes of the slice: x: 2, y: 2, z: 4, core: 2. Of those that a mesh axis runs over, the one named last changes fastest.
Arguments:
- hidden_input: bfloat16 [256, 8192], P(None, 'ctx'), may hold values from -6 to 6
- w_query: bfloat16 [8192, 8192], P('ctx', 'tp')
- key_value_weight: bfloat16 [8192, 2, 1024], P('ctx', None, 'tp'), may hold values from -0.0625 to 0.0625
- w_out: bfloat16 [8192, 8192], P('tp', 'ctx'), may hold values from -0.0625 to 0.0625
- key_value_cache: bfloat16 [2, 8, 32768, 128], P(None, 'tp', 'ctx'), may hold values from -6 to 6
- filled: int32 [8], P('ctx'), may hold values from 512 to 4096, as said below
- positions: int32 [256], replicated, may hold values from 0 to 255, each once
Outputs:
- layer_out: bfloat16 [256, 8192], P('tp', 'ctx')
Inputs may be any that keep to these rules, and one draw needn't show every extreme that they name: `filled`: every shard has at least 512 used slots; some shard is full and some holds exactly 512.
All inputs are finite; a program needn't handle non-finite values.
Results may differ from a plain program's by a relative error of at most 0.0045.
The roundings to bfloat16 on the way count: a program that leaves them out, or rounds other values in their place, can miss the bound.
Values may be sent and summed in bfloat16 or wider, within the bound.
A program may use at most 128 MiB of HBM per device.

v0:
```python
import math

import jax
import jax.numpy as jnp
from jax import lax
from jax.sharding import PartitionSpec as P

NEG_FILL = -1e30


def cache_attend(query_rows, key_rows, val_rows, filled_now, inv_root):
    slots = key_rows.shape[1]
    block = math.gcd(slots, 1024)
    blocks = slots // block

    def block_step(block_idx, carry):
        row_max, denom, accum = carry
        key_block = lax.dynamic_slice_in_dim(key_rows, block_idx * block, block, 1)
        val_block = lax.dynamic_slice_in_dim(val_rows, block_idx * block, block, 1)
        scores = (
            jnp.einsum("kgrd,ksd->kgrs", query_rows, key_block, preferred_element_type=jnp.float32)
            * inv_root
        )
        places = block_idx * block + jnp.arange(block, dtype=jnp.int32)
        scores = jnp.where(places < filled_now, scores, NEG_FILL)
        new_max = jnp.maximum(row_max, jnp.max(scores, axis=-1))
        rescale = jnp.exp(row_max - new_max)
        probs = jnp.exp(scores - new_max[..., None])
        update = jnp.einsum(
            "kgrs,ksd->kgrd",
            probs.astype(jnp.bfloat16),
            val_block,
            preferred_element_type=jnp.float32,
        )
        accum = accum * rescale[..., None] + update
        denom = denom * rescale + jnp.sum(probs, axis=-1)
        return (new_max, denom, accum)

    start = (
        jnp.full(query_rows.shape[:3], NEG_FILL, jnp.float32),
        jnp.zeros(query_rows.shape[:3], jnp.float32),
        jnp.zeros(query_rows.shape, jnp.float32),
    )
    row_max, denom, accum = lax.fori_loop(0, blocks, block_step, start)
    return (row_max + jnp.log(denom), accum / denom[..., None])


def block_attend(query_rows, key_rows, val_rows, causal_mask, inv_root):
    scores = (
        jnp.einsum("kgrd,ksd->kgrs", query_rows, key_rows, preferred_element_type=jnp.float32)
        * inv_root
    )
    scores = jnp.where(causal_mask[None, None], scores, NEG_FILL)
    row_max = jnp.max(scores, axis=-1)
    probs = jnp.exp(scores - row_max[..., None])
    denom = jnp.sum(probs, axis=-1)
    accum = jnp.einsum(
        "kgrs,ksd->kgrd", probs.astype(jnp.bfloat16), val_rows, preferred_element_type=jnp.float32
    )
    return (row_max + jnp.log(denom), accum / denom[..., None])


def to_tokens(log_sums, outputs):
    row_count = log_sums.shape[2]
    head_dim = outputs.shape[3]
    return (
        log_sums.reshape(-1, row_count).T,
        jnp.transpose(outputs.reshape(-1, row_count, head_dim), (1, 0, 2)),
    )


def body(hidden_input, w_query, key_value_weight, w_out, key_value_cache, filled, positions):
    tokens = hidden_input.shape[0]
    shards = lax.axis_size("ctx")
    own_rows = tokens // shards
    kv_heads = key_value_cache.shape[1]
    head_dim = key_value_cache.shape[3]
    q_heads = w_query.shape[1] // head_dim
    group_size = q_heads // kv_heads
    width_loc = w_query.shape[0]
    inv_root = 1.0 / math.sqrt(head_dim)
    w_in = jnp.concatenate([w_query, key_value_weight.reshape(width_loc, -1)], axis=1)
    projected_all = lax.psum(
        jnp.dot(hidden_input, w_in, preferred_element_type=jnp.float32), "ctx"
    ).astype(jnp.bfloat16)
    query_cols = q_heads * head_dim
    kv_cols = kv_heads * head_dim
    query_rows = jnp.transpose(
        projected_all[:, :query_cols].reshape(tokens, kv_heads, group_size, head_dim), (1, 2, 0, 3)
    )
    new_keys = jnp.transpose(
        projected_all[:, query_cols : query_cols + kv_cols].reshape(tokens, kv_heads, head_dim),
        (1, 0, 2),
    )
    new_vals = jnp.transpose(
        projected_all[:, query_cols + kv_cols :].reshape(tokens, kv_heads, head_dim), (1, 0, 2)
    )
    cache_log, cache_out = to_tokens(
        *cache_attend(query_rows, key_value_cache[0], key_value_cache[1], filled[0], inv_root)
    )
    log_parts, out_parts = (
        lax.all_to_all(cache_log[None], "ctx", split_axis=1, concat_axis=0, tiled=True),
        lax.all_to_all(cache_out[None], "ctx", split_axis=1, concat_axis=0, tiled=True),
    )
    first_own = lax.axis_index("ctx") * own_rows
    own_queries = lax.dynamic_slice_in_dim(query_rows, first_own, own_rows, 2)
    own_positions = lax.dynamic_slice_in_dim(positions, first_own, own_rows, 0)
    causal_mask = positions[None, :] <= own_positions[:, None]
    new_log, new_out = to_tokens(
        *block_attend(own_queries, new_keys, new_vals, causal_mask, inv_root)
    )
    all_log = jnp.concatenate([log_parts, new_log[None]], axis=0)
    all_out = jnp.concatenate([out_parts, new_out[None]], axis=0)
    top_log = jnp.max(all_log, axis=0)
    shares = jnp.exp(all_log - top_log[None])
    merged = jnp.sum(shares[..., None] * all_out, axis=0) / jnp.sum(shares, axis=0)[..., None]
    attended = merged.astype(jnp.bfloat16).reshape(own_rows, query_cols)
    part_out = jnp.dot(
        lax.all_gather(attended, "ctx", axis=0, tiled=True),
        w_out,
        preferred_element_type=jnp.float32,
    )
    return lax.psum_scatter(part_out, "tp", scatter_dimension=0, tiled=True).astype(jnp.bfloat16)


def solution(mesh):
    placed = (
        P(None, "ctx"),
        P("ctx", "tp"),
        P("ctx", None, "tp"),
        P("tp", "ctx"),
        P(None, "tp", "ctx", None),
        P("ctx"),
        P(),
    )
    return jax.shard_map(
        body, mesh=mesh, in_specs=placed, out_specs=P("tp", "ctx"), check_vma=False
    )
```

profile of v0, /device:TPU:1, one launch (start us, length us, event | category | flops | bytes accessed | tf_op | source)
XLA Modules:
  0.0 339.4 jit_solution(6594446714789034644)
XLA Ops:
  6.5 1.5 copy.66
  8.1 5.3 %fusion.23 = f32[256,2560]{0,1:T(8,128)} fusion(bf16[256,1024]{1,0:T(8,128)(2,1)S(1)} %copy-done, bf16[1024,512]{1,0:T(8,128)(2,1)S(1)} %bitcast.114, bf16[1024,2048]{1,0:T(8,128)(2,1)} %param.10), kind=kOutput, calls=%fused_computation.28 | convolution fusion | flops 1352663040 | bytes 8388608 | tf_op jit(solution)/shard_map/dot_general | solution.py:84
  13.4 105.9 %all-reduce.1 = bf16[256,2560]{0,1:T(8,128)(2,1)S(1)} all-reduce(f32[256,2560]{0,1:T(8,128)} %fusion.23), channel_id=1, replica_groups=mesh['ctx'=8,'tp'=4] {'ctx'}, use_global_device_ids=true, to_apply=%region_0.0 | all-reduce | flops 655360 | bytes 3932160 | tf_op jit(solution)/shard_map/psum | solution.py:83
  120.3 1.6 copy.48
  121.9 4.4 %slice_bitcast_fusion = (bf16[2,4096,128]{2,1,0:T(8,128)(2,1)}, bf16[2,4096,128]{2,1,0:T(8,128)(2,1)}) fusion(bf16[2,2,4096,128]{3,2,1,0:T(8,128)(2,1)} %param.13), kind=kLoop, calls=%fused_computation.32 | loop fusion | bytes 8388608 | tf_op jit(solution)/shard_map/squeeze | solution.py:99
  126.3 66.4 %while.18 = (s32[]{:T(128)}, f32[2,8,256]{2,1,0:T(8,128)S(1)}, f32[2,8,256]{2,1,0:T(8,128)S(1)}, f32[2,8,256,128]{3,2,1,0:T(8,128)}, s32[]{:T(128)}, /*index=5*/...) while((s32[]{:T(128)}, f32[2,8,256]{2,1,0:T(8,128)S(1)}, ...), condition=%wide.region_4.5_spmd.clone, body=%wide.region_1.4_spmd.clone.sunk | while | flops 2195216384 | bytes 73666816 | solution.py:44
  127.0 3.8 %bitcast_reduce_fusion.2 = (f32[2,8,256]{2,1,0:T(8,128)S(1)}, f32[2,1024,8,256]{3,1,2,0:T(8,128)S(1)}) fusion(pred[1024]{0:T(1024)(128)(4,1)S(1)} %add_compare_fusion.2, bf16[2,8,256,128]{3,2,1,0:T(8,128)(2,1)S(1)} %get-tuple-element.291, bf16[2,4096,128]{2,1,0:T(8,128)(2,1)} %get-tuple-element.290, s32[]{:T(128)S(6)} %select_n.52), kind=kOutput, calls=%fused_computation.1.clone.1 | convolution fusion | flops 1086320640 | bytes 18367492 | tf_op jit(solution)/shard_map/while/body/eval_jaxpr/kgrd,ksd->kgrs/dot_general | solution.py:21
  130.8 4.1 %fusion.58 = f32[2,8,256]{2,1,0:T(8,128)S(1)} fusion(f32[2,1024,8,256]{3,1,2,0:T(8,128)S(1)} %get-tuple-element.258, f32[2,8,256]{2,1,0:T(8,128)S(1)} %select_maximum_fusion.2, pred[1024]{0:T(1024)(128)(4,1)S(1)} %add_compare_fusion.2), kind=kLoop, calls=%fused_computation.5.clone.1 | loop fusion | flops 16773120 | bytes 16811008 | tf_op jit(solution)/shard_map/while/body/eval_jaxpr/reduce_sum | solution.py:36
  134.9 6.7 %fusion.60 = f32[2,8,256,128]{3,2,1,0:T(8,128)S(1)} fusion(f32[2,8,256,128]{3,2,1,0:T(8,128)S(1)} %copy-done.1, f32[2,1024,8,256]{3,1,2,0:T(8,128)S(1)} %get-tuple-element.258, f32[2,8,256]{2,1,0:T(8,128)S(1)} %select_maximum_fusion.2, pred[1024]{0:T(1024)(128)(4,1)S(1)} %add_compare_fusion.2, f32[2,8,256]{2,1,0:T(8,128)S(1)} %get-tuple-element.260, ...), kind=kOutput, calls=%fused_computation.9.clone.1 | convolution fusion | flops 1092091904 | bytes 21529604 | tf_op jit(solution)/shard_map/while/body/eval_jaxpr/kgrs,ksd->kgrd/dot_general | solution.py:29
  141.6 1.3 copy-done.2
  143.6 3.8 %bitcast_reduce_fusion.2 = (f32[2,8,256]{2,1,0:T(8,128)S(1)}, f32[2,1024,8,256]{3,1,2,0:T(8,128)S(1)}) fusion(pred[1024]{0:T(1024)(128)(4,1)S(1)} %add_compare_fusion.2, bf16[2,8,256,128]{3,2,1,0:T(8,128)(2,1)S(1)} %get-tuple-element.291, bf16[2,4096,128]{2,1,0:T(8,128)(2,1)} %get-tuple-element.290, s32[]{:T(128)S(6)} %select_n.52), kind=kOutput, calls=%fused_computation.1.clone.1 | convolution fusion | flops 1086320640 | bytes 18367492 | tf_op jit(solution)/shard_map/while/body/eval_jaxpr/kgrd,ksd->kgrs/dot_general | solution.py:21
  147.4 4.1 %fusion.58 = f32[2,8,256]{2,1,0:T(8,128)S(1)} fusion(f32[2,1024,8,256]{3,1,2,0:T(8,128)S(1)} %get-tuple-element.258, f32[2,8,256]{2,1,0:T(8,128)S(1)} %select_maximum_fusion.2, pred[1024]{0:T(1024)(128)(4,1)S(1)} %add_compare_fusion.2), kind=kLoop, calls=%fused_computation.5.clone.1 | loop fusion | flops 16773120 | bytes 16811008 | tf_op jit(solution)/shard_map/while/body/eval_jaxpr/reduce_sum | solution.py:36
  151.5 6.7 %fusion.60 = f32[2,8,256,128]{3,2,1,0:T(8,128)S(1)} fusion(f32[2,8,256,128]{3,2,1,0:T(8,128)S(1)} %copy-done.1, f32[2,1024,8,256]{3,1,2,0:T(8,128)S(1)} %get-tuple-element.258, f32[2,8,256]{2,1,0:T(8,128)S(1)} %select_maximum_fusion.2, pred[1024]{0:T(1024)(128)(4,1)S(1)} %add_compare_fusion.2, f32[2,8,256]{2,1,0:T(8,128)S(1)} %get-tuple-element.260, ...), kind=kOutput, calls=%fused_computation.9.clone.1 | convolution fusion | flops 1092091904 | bytes 21529604 | tf_op jit(solution)/shard_map/while/body/eval_jaxpr/kgrs,ksd->kgrd/dot_general | solution.py:29
  158.2 1.3 copy-done.2
  160.2 3.8 %bitcast_reduce_fusion.2 = (f32[2,8,256]{2,1,0:T(8,128)S(1)}, f32[2,1024,8,256]{3,1,2,0:T(8,128)S(1)}) fusion(pred[1024]{0:T(1024)(128)(4,1)S(1)} %add_compare_fusion.2, bf16[2,8,256,128]{3,2,1,0:T(8,128)(2,1)S(1)} %get-tuple-element.291, bf16[2,4096,128]{2,1,0:T(8,128)(2,1)} %get-tuple-element.290, s32[]{:T(128)S(6)} %select_n.52), kind=kOutput, calls=%fused_computation.1.clone.1 | convolution fusion | flops 1086320640 | bytes 18367492 | tf_op jit(solution)/shard_map/while/body/eval_jaxpr/kgrd,ksd->kgrs/dot_general | solution.py:21
  163.9 4.1 %fusion.58 = f32[2,8,256]{2,1,0:T(8,128)S(1)} fusion(f32[2,1024,8,256]{3,1,2,0:T(8,128)S(1)} %get-tuple-element.258, f32[2,8,256]{2,1,0:T(8,128)S(1)} %select_maximum_fusion.2, pred[1024]{0:T(1024)(128)(4,1)S(1)} %add_compare_fusion.2), kind=kLoop, calls=%fused_computation.5.clone.1 | loop fusion | flops 16773120 | bytes 16811008 | tf_op jit(solution)/shard_map/while/body/eval_jaxpr/reduce_sum | solution.py:36
  168.1 6.7 %fusion.60 = f32[2,8,256,128]{3,2,1,0:T(8,128)S(1)} fusion(f32[2,8,256,128]{3,2,1,0:T(8,128)S(1)} %copy-done.1, f32[2,1024,8,256]{3,1,2,0:T(8,128)S(1)} %get-tuple-element.258, f32[2,8,256]{2,1,0:T(8,128)S(1)} %select_maximum_fusion.2, pred[1024]{0:T(1024)(128)(4,1)S(1)} %add_compare_fusion.2, f32[2,8,256]{2,1,0:T(8,128)S(1)} %get-tuple-element.260, ...), kind=kOutput, calls=%fused_computation.9.clone.1 | convolution fusion | flops 1092091904 | bytes 21529604 | tf_op jit(solution)/shard_map/while/body/eval_jaxpr/kgrs,ksd->kgrd/dot_general | solution.py:29
  174.8 1.3 copy-done.2
  176.7 3.8 %bitcast_reduce_fusion.2 = (f32[2,8,256]{2,1,0:T(8,128)S(1)}, f32[2,1024,8,256]{3,1,2,0:T(8,128)S(1)}) fusion(pred[1024]{0:T(1024)(128)(4,1)S(1)} %add_compare_fusion.2, bf16[2,8,256,128]{3,2,1,0:T(8,128)(2,1)S(1)} %get-tuple-element.291, bf16[2,4096,128]{2,1,0:T(8,128)(2,1)} %get-tuple-element.290, s32[]{:T(128)S(6)} %select_n.52), kind=kOutput, calls=%fused_computation.1.clone.1 | convolution fusion | flops 1086320640 | bytes 18367492 | tf_op jit(solution)/shard_map/while/body/eval_jaxpr/kgrd,ksd->kgrs/dot_general | solution.py:21
  180.5 4.1 %fusion.58 = f32[2,8,256]{2,1,0:T(8,128)S(1)} fusion(f32[2,1024,8,256]{3,1,2,0:T(8,128)S(1)} %get-tuple-element.258, f32[2,8,256]{2,1,0:T(8,128)S(1)} %select_maximum_fusion.2, pred[1024]{0:T(1024)(128)(4,1)S(1)} %add_compare_fusion.2), kind=kLoop, calls=%fused_computation.5.clone.1 | loop fusion | flops 16773120 | bytes 16811008 | tf_op jit(solution)/shard_map/while/body/eval_jaxpr/reduce_sum | solution.py:36
  184.7 6.7 %fusion.60 = f32[2,8,256,128]{3,2,1,0:T(8,128)S(1)} fusion(f32[2,8,256,128]{3,2,1,0:T(8,128)S(1)} %copy-done.1, f32[2,1024,8,256]{3,1,2,0:T(8,128)S(1)} %get-tuple-element.258, f32[2,8,256]{2,1,0:T(8,128)S(1)} %select_maximum_fusion.2, pred[1024]{0:T(1024)(128)(4,1)S(1)} %add_compare_fusion.2, f32[2,8,256]{2,1,0:T(8,128)S(1)} %get-tuple-element.260, ...), kind=kOutput, calls=%fused_computation.9.clone.1 | convolution fusion | flops 1092091904 | bytes 21529604 | tf_op jit(solution)/shard_map/while/body/eval_jaxpr/kgrs,ksd->kgrd/dot_general | solution.py:29
  191.4 1.3 copy-done.2
  194.9 5.5 %all-to-all-start = ((f32[8,1,512]{2,1,0:T(1,128)}), f32[8,1,512]{2,1,0:T(1,128)S(1)}, u32[]{:S(2)}, u32[]{:S(2)}) async-start(f32[8,1,512]{2,1,0:T(1,128)} %reshape.106), calls=%async_computation | async-start | bytes 32768 | tf_op jit(solution)/shard_map/all_to_all | solution.py:102
  200.5 1.9 broadcast_divide_fusion
  202.4 2.5 copy.69
  205.9 4.5 %all-to-all-start.1 = ((f32[1,256,16,128]{3,2,0,1:T(8,128)}), f32[1,256,16,128]{3,2,0,1:T(8,128)}, u32[]{:S(2)}, u32[]{:S(2)}) async-start(f32[1,256,16,128]{3,2,0,1:T(8,128)} %bitcast.109), calls=%async_computation.1 | async-start | bytes 4194304 | tf_op jit(solution)/shard_map/all_to_all | solution.py:103
  213.1 43.6 %all-to-all-done.1 = f32[1,256,16,128]{3,2,0,1:T(8,128)} async-done(((f32[1,256,16,128]{3,2,0,1:T(8,128)}), f32[1,256,16,128]{3,2,0,1:T(8,128)}, u32[]{:S(2)}, u32[]{:S(2)}) %all-to-all-start.1) | async-done | bytes 2097184 | tf_op jit(solution)/shard_map/all_to_all | solution.py:103
  256.7 2.3 copy.58
  260.6 40.7 %all-gather.2.cloned.1.call-done = bf16[256,2048]{1,0:T(8,128)(2,1)} async-done(((bf16[32,2048]{1,0:T(8,128)(2,1)}), bf16[256,2048]{1,0:T(8,128)(2,1)}) %all-gather.2.cloned.1.call-update) | async-done | bytes 1048592 | tf_op jit(solution)/shard_map/all_gather | solution.py:119
  301.3 4.8 %fusion.43 = f32[256,1024]{1,0:T(8,128)} fusion(bf16[256,2048]{1,0:T(8,128)(2,1)} %all-gather.2.cloned.1.call-done, bf16[2048,1024]{1,0:T(8,128)(2,1)} %param.12), kind=kOutput, calls=%fused_computation.60 | convolution fusion | flops 1073741824 | bytes 6291456 | tf_op jit(solution)/shard_map/dot_general | solution.py:118
  306.1 24.8 %reduce-scatter.2.cloned.1.call-done = f32[64,1024]{1,0:T(8,128)} async-done(((f32[256,1024]{1,0:T(8,128)}), f32[64,1024]{1,0:T(8,128)}) %reduce-scatter.2.cloned.1.call-update) | async-done | bytes 262160 | tf_op jit(solution)/shard_map/reduce_scatter | solution.py:123
  330.9 1.6 convert_element_type.27
  (66 shorter events, 11.2 us)
Async XLA Ops:
  6.5 1.5 copy-start
  130.8 4.1 %copy-start.1 = (f32[2,8,256,128]{3,2,1,0:T(8,128)S(1)}, f32[2,8,256,128]{3,2,1,0:T(8,128)}, u32[]{:S(2)}) copy-start(f32[2,8,256,128]{3,2,1,0:T(8,128)} %get-tuple-element.276) | copy-start | bytes 6291460 | tf_op jit(solution)/shard_map/while
  141.6 1.3 copy-start.2
  147.4 4.1 %copy-start.1 = (f32[2,8,256,128]{3,2,1,0:T(8,128)S(1)}, f32[2,8,256,128]{3,2,1,0:T(8,128)}, u32[]{:S(2)}) copy-start(f32[2,8,256,128]{3,2,1,0:T(8,128)} %get-tuple-element.276) | copy-start | bytes 6291460 | tf_op jit(solution)/shard_map/while
  158.2 1.3 copy-start.2
  163.9 4.1 %copy-start.1 = (f32[2,8,256,128]{3,2,1,0:T(8,128)S(1)}, f32[2,8,256,128]{3,2,1,0:T(8,128)}, u32[]{:S(2)}) copy-start(f32[2,8,256,128]{3,2,1,0:T(8,128)} %get-tuple-element.276) | copy-start | bytes 6291460 | tf_op jit(solution)/shard_map/while
  174.8 1.3 copy-start.2
  180.5 4.1 %copy-start.1 = (f32[2,8,256,128]{3,2,1,0:T(8,128)S(1)}, f32[2,8,256,128]{3,2,1,0:T(8,128)}, u32[]{:S(2)}) copy-start(f32[2,8,256,128]{3,2,1,0:T(8,128)} %get-tuple-element.276) | copy-start | bytes 6291460 | tf_op jit(solution)/shard_map/while
  191.4 1.3 copy-start.2
  194.9 11.0 %all-to-all-start = ((f32[8,1,512]{2,1,0:T(1,128)}), f32[8,1,512]{2,1,0:T(1,128)S(1)}, u32[]{:S(2)}, u32[]{:S(2)}) async-start(f32[8,1,512]{2,1,0:T(1,128)} %reshape.106), calls=%async_computation | async-start | bytes 32768 | tf_op jit(solution)/shard_map/all_to_all | solution.py:102
  202.4 8.3 %copy-start.3 = (s32[256]{0:T(256)S(1)}, s32[256]{0:T(256)}, u32[]{:S(2)}) copy-start(s32[256]{0:T(256)} %param.15) | copy-start | bytes 3076
  205.9 50.8 %all-to-all-start.1 = ((f32[1,256,16,128]{3,2,0,1:T(8,128)}), f32[1,256,16,128]{3,2,0,1:T(8,128)}, u32[]{:S(2)}, u32[]{:S(2)}) async-start(f32[1,256,16,128]{3,2,0,1:T(8,128)} %bitcast.109), calls=%async_computation.1 | async-start | bytes 4194304 | tf_op jit(solution)/shard_map/all_to_all | solution.py:103
  210.4 90.9 %all-gather.2.cloned.1.call-start = ((), (), s32[]{:S(2)}) async-start(), calls=%async_computation.3 | async-start | bytes 1179648 | tf_op jit(solution)/shard_map/all_gather | solution.py:119
  260.6 70.3 %reduce-scatter.2.cloned.1.call-start = ((), (), s32[]{:S(2)}) async-start(), calls=%async_computation.4 | async-start | bytes 1310720 | tf_op jit(solution)/shard_map/reduce_scatter | solution.py:123
Sparse Core Ops, SparseCore 0:
  260.7 40.5 all-gather.1
  306.2 24.6 reduce-scatter.1
where the time goes:
time: 341 us; the launch traced here: 339 us
  waiting for transfers between devices  110 us (32%)
  blocking collectives  106 us (31%)
  matrix products  52.4 us (15%)
  other arithmetic  26.1 us (8%)
  local copies, waits for them, and re-layouts  20.9 us (6%)
  between operations  13.6 us (4%)
  starting transfers between devices  10.1 us (3%)
    psum x1, blocking collectives, body(): lax.psum(jnp.dot(hidden_input, w_in, preferred_element_type=jnp.float32),...  106 us
    all_to_all x1, waiting for transfers between devices, body(): lax.all_to_all(cache_out[None], 'ctx', split_axis=1, concat_axis=0, tiled...  43.6 us
    all_gather x1, waiting for transfers between devices, body(): lax.all_gather(attended, 'ctx', axis=0, tiled=True)  40.7 us
    dot_general x4, matrix products, block_step(): jnp.einsum('kgrs,ksd->kgrd', probs.astype(jnp.bfloat16), val_block, prefe...  26.7 us
    reduce_scatter x1, waiting for transfers between devices, body(): lax.psum_scatter(part_out, 'tp', scatter_dimension=0, tiled=True)  24.8 us
    reduce_sum x4, other arithmetic, block_step(): denom = denom * rescale + jnp.sum(probs, axis=-1)  16.3 us
    dot_general x4, matrix products, block_step(): jnp.einsum('kgrd,ksd->kgrs', query_rows, key_block, preferred_element_typ...  15 us
  transfers between devices with their start and end apart: 4, of which 4 were waited for; matrix products, arithmetic and copies ran while one was open for 2% of the time, Pallas kernels for 0%

commit v1 on v0

v1 whole, which is shorter than its diff:
```python
import functools
import math

import jax
import jax.numpy as jnp
from jax import lax
from jax.experimental import pallas as pl
from jax.experimental.pallas import tpu as pltpu
from jax.sharding import PartitionSpec as P

MESH = pl.DeviceIdType.MESH
HIDE = -1e30
LOG2E = 1.4426950408889634


def factor(shards):
    for inner in (8, 2) if shards > 8 else (2,):
        if shards % inner == 0:
            return shards // inner, inner
    return shards, 1


def greet(peers):
    barrier = pltpu.get_barrier_semaphore()
    for peer in peers:
        pl.semaphore_signal(barrier, inc=1, device_id=peer, device_id_type=MESH)
    pl.semaphore_wait(barrier, len(peers))


def peers_of(outer, inner):
    me = lax.axis_index("ctx")
    z = me // inner
    x = me % inner
    xs = [(x + d) % inner for d in range(1, inner)]
    zs = [(z + d) % outer for d in range(1, outer)]
    x_ids = [{"ctx": z * inner + v} for v in xs]
    z_ids = [{"ctx": v * inner + x} for v in zs]
    return x, z, xs, zs, x_ids, z_ids


def remote(src, dst, sems, place, peer):
    return pltpu.make_async_remote_copy(
        src_ref=src,
        dst_ref=dst,
        send_sem=sems[0].at[place],
        recv_sem=sems[1].at[place],
        device_id=peer,
        device_id_type=MESH,
    )


def project_kernel(
    outer, inner, q_blocks,
    hid_ref, wq_ref, wkv_ref,
    q_ref, kv_ref,
    w_buf, part_x, recv_x, acc, recv_z,
    w_sem, sx, rx, sz, rz, gz, hz, gx, hx,
):
    blocks = q_blocks + 1
    rows = acc.shape[2]
    cols = acc.shape[3]
    x, z, xs, zs, x_ids, z_ids = peers_of(outer, inner)
    loads = []
    for b in range(blocks):
        src = wq_ref.at[:, pl.ds(b * cols, cols)] if b < q_blocks else wkv_ref
        load = pltpu.make_async_copy(src, w_buf.at[b], w_sem.at[b])
        load.start()
        loads.append(load)
    greet(x_ids + z_ids)
    def ship(b):
        loads[b].wait()
        copies = []
        for d, peer in enumerate(x_ids):
            part_x[b, d] = jnp.dot(
                hid_ref[xs[d]], w_buf[b], preferred_element_type=jnp.float32
            )
            copy = remote(part_x.at[b, d], recv_x.at[b, d], (sx, rx), (b, d), peer)
            copy.start()
            copies.append(copy)
        own = jnp.dot(hid_ref[x], w_buf[b], preferred_element_type=jnp.float32)
        acc[b] = own.reshape(outer, rows, cols)
        return copies

    def add_x(b, x_copies):
        copies = []
        for copy in x_copies:
            copy.wait_recv()
        total = acc[b]
        for d in range(inner - 1):
            total += recv_x[b, d].reshape(outer, rows, cols)
        acc[b] = total
        for d, peer in enumerate(z_ids):
            copy = remote(acc.at[b, zs[d]], recv_z.at[b, d], (sz, rz), (b, d), peer)
            copy.start()
            copies.append(copy)
        return copies

    def add_z(b, z_copies):
        for copy in z_copies:
            copy.wait_recv()
        total = acc[b, z]
        for d in range(outer - 1):
            total += recv_z[b, d]
        low = total.astype(jnp.bfloat16)
        copies = []
        if b == q_blocks:
            kv_ref[...] = low
            return copies
        q_ref[b, x, z] = low
        for d, peer in enumerate(z_ids):
            copy = remote(q_ref.at[b, x, z], q_ref.at[b, x, z], (gz, hz), (b, d), peer)
            copy.start()
            copies.append(copy)
        return copies

    def spread(b, z_copies):
        copies = []
        for copy in z_copies:
            copy.wait_recv()
        for d, peer in enumerate(x_ids):
            copy = remote(q_ref.at[b, x], q_ref.at[b, x], (gx, hx), (b, d), peer)
            copy.start()
            copies.append(copy)
        return copies

    first = [ship(b) for b in range(blocks)]
    second, third, fourth = {}, {}, {}
    for t in range(blocks + 2):
        if t < blocks:
            second[t] = add_x(t, first[t])
        if 0 <= t - 1 < blocks:
            third[t - 1] = add_z(t - 1, second[t - 1])
        if 0 <= t - 2 < q_blocks:
            fourth[t - 2] = spread(t - 2, third[t - 2])
    for b in range(q_blocks):
        for copy in fourth[b]:
            copy.wait_recv()
    for group in (first, list(second.values()), list(third.values()), list(fourth.values())):
        for copies in group:
            for copy in copies:
                copy.wait_send()


def project(hidden, w_query, w_kv, outer, inner):
    tokens, width = hidden.shape
    shards = outer * inner
    rows = tokens // shards
    cols = w_kv.shape[1]
    q_blocks = w_query.shape[1] // cols
    blocks = q_blocks + 1
    dma = pltpu.SemaphoreType.DMA
    vmem = pl.BlockSpec(memory_space=pltpu.VMEM)
    hbm = pl.BlockSpec(memory_space=pl.ANY)
    nx, nz = max(inner - 1, 1), max(outer - 1, 1)
    return pl.pallas_call(
        functools.partial(project_kernel, outer, inner, q_blocks),
        out_shape=(
            jax.ShapeDtypeStruct((q_blocks, inner, outer, rows, cols), jnp.bfloat16),
            jax.ShapeDtypeStruct((rows, cols), jnp.bfloat16),
        ),
        in_specs=[vmem, hbm, hbm],
        out_specs=(vmem, vmem),
        scratch_shapes=[
            pltpu.VMEM((blocks, width, cols), jnp.bfloat16),
            pltpu.VMEM((blocks, nx, outer * rows, cols), jnp.float32),
            pltpu.VMEM((blocks, nx, outer * rows, cols), jnp.float32),
            pltpu.VMEM((blocks, outer, rows, cols), jnp.float32),
            pltpu.VMEM((blocks, nz, rows, cols), jnp.float32),
            dma((blocks,)),
            dma((blocks, nx)), dma((blocks, nx)),
            dma((blocks, nz)), dma((blocks, nz)),
            dma((q_blocks, nz)), dma((q_blocks, nz)),
            dma((q_blocks, nx)), dma((q_blocks, nx)),
        ],
        compiler_params=pltpu.CompilerParams(
            collective_id=0, has_side_effects=True, vmem_limit_bytes=48 << 20
        ),
        name="project",
    )(hidden.reshape(inner, outer * rows, width), w_query, w_kv)


def attend_kernel(
    scale, kb,
    filled_ref, q_ref, k_ref, v_ref, kn_ref, vn_ref, posq_ref, posk_ref,
    o_ref, lse_ref,
    k_aug, v_aug, score,
):
    g, h = pl.program_id(0), pl.program_id(1)
    slots = k_ref.shape[2]
    tokens, dim = q_ref.shape[1], q_ref.shape[2]
    extra = posk_ref.shape[1]
    filled = filled_ref[0]
    lane = lax.broadcasted_iota(jnp.int32, (1, dim), 1)

    @pl.when((g == 0) & (h == 0))
    def _():
        lse_ref[...] = jnp.zeros_like(lse_ref)

    @pl.when(h == 0)
    def _():
        k_aug[:, :dim] = k_ref[0, 0]
        v_aug[:slots, :dim] = v_ref[0, 0]
        row = lax.broadcasted_iota(jnp.int32, (slots, dim), 0)
        col = lax.broadcasted_iota(jnp.int32, (slots, dim), 1)
        k_aug[:, dim:] = jnp.where(
            (row >= filled) & (col == 0), HIDE, 0.0
        ).astype(jnp.bfloat16)
        v_aug[slots:, :] = jnp.zeros((extra, 2 * dim), jnp.bfloat16)
        v_aug[slots : slots + kn_ref.shape[0], :dim] = vn_ref[...]
        v_aug[:, dim:] = jnp.where(
            lax.broadcasted_iota(jnp.int32, (slots + extra, dim), 1) == 0, 1.0, 0.0
        ).astype(jnp.bfloat16)

    q = q_ref[0]
    q_aug = jnp.concatenate(
        [q, jnp.broadcast_to(jnp.where(lane == 0, 1.0, 0.0).astype(jnp.bfloat16), q.shape)], axis=1
    )
    nt = (((1,), (1,)), ((), ()))
    kn = jnp.concatenate(
        [kn_ref[...], jnp.zeros((extra - kn_ref.shape[0], dim), jnp.bfloat16)], axis=0
    ) if extra > kn_ref.shape[0] else kn_ref[...]
    fresh = lax.dot_general(q, kn, nt, preferred_element_type=jnp.float32)
    fresh = jnp.where(posk_ref[...] <= posq_ref[...], fresh, HIDE)
    score[:, slots:] = fresh
    top = fresh
    for b in range(slots // kb):
        part = lax.dot_general(
            q_aug, k_aug[b * kb : (b + 1) * kb, :], nt, preferred_element_type=jnp.float32
        )
        score[:, b * kb : (b + 1) * kb] = part
        for j in range(kb // dim):
            top = jnp.maximum(top, part[:, j * dim : (j + 1) * dim])
    peak = jnp.max(top, axis=1, keepdims=True)
    shift = peak * (scale * LOG2E)
    total = None
    for b in range(slots // kb + 1):
        lo = b * kb
        hi = min(lo + kb, slots + extra)
        probs = jnp.exp2(score[:, lo:hi] * (scale * LOG2E) - shift).astype(jnp.bfloat16)
        term = jnp.dot(probs, v_aug[lo:hi, :], preferred_element_type=jnp.float32)
        total = term if total is None else total + term
    denom = total[:, dim : dim + 1]
    o_ref[0] = (total[:, :dim] / denom).astype(o_ref.dtype)
    head = g * pl.num_programs(1) + h
    lse_ref[...] = jnp.where(lane == head, peak * scale + jnp.log(denom), lse_ref[...])


def attend(q, kv_new, cache, filled, positions, own_positions, scale):
    q_blocks, tokens, cols = q.shape
    _, kv_heads, slots, dim = cache.shape
    per = cols // dim
    group = q_blocks * per // kv_heads
    rows = kv_new.shape[0]
    extra = 128
    padded = jnp.concatenate(
        [own_positions, jnp.full((extra - rows,), tokens + 1, jnp.int32)]
    )
    once = pl.BlockSpec((tokens, 1), lambda g, h: (0, 0))
    return pl.pallas_call(
        functools.partial(attend_kernel, scale, math.gcd(slots, 512)),
        grid=(kv_heads, group),
        out_shape=(
            jax.ShapeDtypeStruct((q_blocks, tokens, cols), jnp.bfloat16),
            jax.ShapeDtypeStruct((tokens, 128), jnp.float32),
        ),
        in_specs=[
            pl.BlockSpec(memory_space=pltpu.SMEM),
            pl.BlockSpec(
                (1, tokens, dim), lambda g, h: ((g * group + h) // per, 0, (g * group + h) % per)
            ),
            pl.BlockSpec((1, 1, slots, dim), lambda g, h: (0, g, 0, 0)),
            pl.BlockSpec((1, 1, slots, dim), lambda g, h: (1, g, 0, 0)),
            pl.BlockSpec((rows, dim), lambda g, h: (0, g)),
            pl.BlockSpec((rows, dim), lambda g, h: (0, kv_heads + g)),
            once,
            pl.BlockSpec((1, extra), lambda g, h: (0, 0)),
        ],
        out_specs=(
            pl.BlockSpec(
                (1, tokens, dim), lambda g, h: ((g * group + h) // per, 0, (g * group + h) % per)
            ),
            pl.BlockSpec((tokens, 128), lambda g, h: (0, 0)),
        ),
        scratch_shapes=[
            pltpu.VMEM((slots, 2 * dim), jnp.bfloat16),
            pltpu.VMEM((slots + extra, 2 * dim), jnp.bfloat16),
            pltpu.VMEM((tokens, slots + extra), jnp.float32),
        ],
        compiler_params=pltpu.CompilerParams(
            dimension_semantics=("arbitrary", "arbitrary"), vmem_limit_bytes=40 << 20
        ),
        name="attend",
    )(
        filled, q, cache, cache, kv_new, kv_new,
        positions.reshape(tokens, 1), padded.reshape(1, extra),
    )


def merge_kernel(
    outer, inner, tp_size, dim,
    o_ref, lse_ref, w_ref,
    out_ref,
    w_buf, att, recv_x, lse_x, mid, mid_lse, recv_z, lse_z, part, part_low, recv_t,
    w_sem, slx, rlx, sx, rx, slz, rlz, sz, rz, gz, hz, gx, hx, st, rt,
):
    blocks = o_ref.shape[0]
    rows = att.shape[3]
    cols = att.shape[4]
    per = cols // dim
    x, z, xs, zs, x_ids, z_ids = peers_of(outer, inner)
    tp = lax.axis_index("tp")
    ts = [(tp + d) % tp_size for d in range(1, tp_size)]
    t_ids = [{"tp": v} for v in ts]
    load = pltpu.make_async_copy(w_ref, w_buf, w_sem)
    load.start()
    greet(x_ids + z_ids + t_ids)
    sent = []

    def go(*args):
        copy = remote(*args)
        copy.start()
        sent.append(copy)
        return copy

    def shares(logs):
        top = functools.reduce(jnp.maximum, logs)
        weights = [jnp.exp(v - top) for v in logs]
        total = sum(weights[1:], weights[0])
        return [w / total for w in weights], top + jnp.log(total)

    def blend(b, weights, values):
        pieces = []
        for j in range(per):
            head = b * per + j
            acc = None
            for w, v in zip(weights, values):
                term = w[:, head : head + 1] * v[:, j * dim : (j + 1) * dim].astype(jnp.float32)
                acc = term if acc is None else acc + term
            pieces.append(acc)
        return jnp.concatenate(pieces, axis=1).astype(jnp.bfloat16)

    lx = [
        go(lse_ref.at[xs[d]], lse_x.at[d], (slx, rlx), d, peer) for d, peer in enumerate(x_ids)
    ]
    ox = [
        [go(o_ref.at[b, xs[d]], recv_x.at[b, d], (sx, rx), (b, d), peer) for d, peer in enumerate(x_ids)]
        for b in range(blocks)
    ]
    for copy in lx:
        copy.wait_recv()
    x_weights, x_log = shares([lse_ref[x]] + [lse_x[d] for d in range(inner - 1)])
    mid_lse[...] = x_log.reshape(outer, rows, 128)
    lz = [
        go(mid_lse.at[zs[d]], lse_z.at[d], (slz, rlz), d, peer) for d, peer in enumerate(z_ids)
    ]
    oz, az, ax = {}, {}, {}
    z_weights = None
    for t in range(blocks + 2):
        if t < blocks:
            b = t
            for copy in ox[b]:
                copy.wait_recv()
            merged = blend(b, x_weights, [o_ref[b, x]] + [recv_x[b, d] for d in range(inner - 1)])
            mid[b] = merged.reshape(outer, rows, cols)
            oz[b] = [
                go(mid.at[b, zs[d]], recv_z.at[b, d], (sz, rz), (b, d), peer)
                for d, peer in enumerate(z_ids)
            ]
        if 0 <= t - 1 < blocks:
            b = t - 1
            if z_weights is None:
                for copy in lz:
                    copy.wait_recv()
                z_weights, _ = shares([mid_lse[z]] + [lse_z[d] for d in range(outer - 1)])
            for copy in oz[b]:
                copy.wait_recv()
            att[b, x, z] = blend(
                b, z_weights, [mid[b, z]] + [recv_z[b, d] for d in range(outer - 1)]
            )
            az[b] = [
                go(att.at[b, x, z], att.at[b, x, z], (gz, hz), (b, d), peer)
                for d, peer in enumerate(z_ids)
            ]
        if 0 <= t - 2 < blocks:
            b = t - 2
            for copy in az[b]:
                copy.wait_recv()
            ax[b] = [
                go(att.at[b, x], att.at[b, x], (gx, hx), (b, d), peer)
                for d, peer in enumerate(x_ids)
            ]
    load.wait()
    half = outer * rows
    for d, v in enumerate([x] + xs):
        for b in range(blocks):
            if d > 0:
                ax[b][inner - 1 - d].wait_recv()
            term = jnp.dot(
                att[b, v].reshape(half, cols),
                w_buf[b * cols : (b + 1) * cols, :],
                preferred_element_type=jnp.float32,
            )
            if b == 0:
                part[v] = term
            else:
                part[v] += term
    share = out_ref.shape[0]
    whole = part[...].reshape(tp_size, share, part.shape[2])
    part_low[...] = whole.astype(jnp.bfloat16)
    rt_copies = [
        go(part_low.at[ts[d]], recv_t.at[d], (st, rt), d, peer) for d, peer in enumerate(t_ids)
    ]
    own = part.reshape(tp_size, share, part.shape[2])[tp]
    for d, copy in enumerate(rt_copies):
        copy.wait_recv()
        own += recv_t[d].astype(jnp.float32)
    out_ref[...] = own.astype(out_ref.dtype)
    for copy in sent:
        copy.wait_send()


def merge(o, lse, w_out, outer, inner, dim):
    blocks, tokens, cols = o.shape
    rows = tokens // (outer * inner)
    half = outer * rows
    tp_size = lax.axis_size("tp")
    width = w_out.shape[1]
    share = tokens // tp_size
    nx, nz, nt = max(inner - 1, 1), max(outer - 1, 1), max(tp_size - 1, 1)
    dma = pltpu.SemaphoreType.DMA
    vmem = pl.BlockSpec(memory_space=pltpu.VMEM)
    low, full = jnp.bfloat16, jnp.float32
    return pl.pallas_call(
        functools.partial(merge_kernel, outer, inner, tp_size, dim),
        out_shape=jax.ShapeDtypeStruct((share, width), low),
        in_specs=[vmem, vmem, pl.BlockSpec(memory_space=pl.ANY)],
        out_specs=vmem,
        scratch_shapes=[
            pltpu.VMEM(w_out.shape, low),
            pltpu.VMEM((blocks, inner, outer, rows, cols), low),
            pltpu.VMEM((blocks, nx, half, cols), low),
            pltpu.VMEM((nx, half, 128), full),
            pltpu.VMEM((blocks, outer, rows, cols), low),
            pltpu.VMEM((outer, rows, 128), full),
            pltpu.VMEM((blocks, nz, rows, cols), low),
            pltpu.VMEM((nz, rows, 128), full),
            pltpu.VMEM((inner, half, width), full),
            pltpu.VMEM((tp_size, share, width), low),
            pltpu.VMEM((nt, share, width), low),
            dma(()),
            dma((nx,)), dma((nx,)),
            dma((blocks, nx)), dma((blocks, nx)),
            dma((nz,)), dma((nz,)),
            dma((blocks, nz)), dma((blocks, nz)),
            dma((blocks, nz)), dma((blocks, nz)),
            dma((blocks, nx)), dma((blocks, nx)),
            dma((nt,)), dma((nt,)),
        ],
        compiler_params=pltpu.CompilerParams(
            collective_id=1, has_side_effects=True, vmem_limit_bytes=48 << 20
        ),
        name="merge",
    )(o.reshape(blocks, inner, half, cols), lse.reshape(inner, half, 128), w_out)


def body(hidden_input, w_query, key_value_weight, w_out, key_value_cache, filled, positions):
    tokens, width = hidden_input.shape
    shards = lax.axis_size("ctx")
    outer, inner = factor(shards)
    rows = tokens // shards
    dim = key_value_cache.shape[3]
    q, kv_new = project(
        hidden_input, w_query, key_value_weight.reshape(width, -1), outer, inner
    )
    me = lax.axis_index("ctx")
    chunk = (me % inner) * outer + me // inner
    own_positions = lax.dynamic_slice_in_dim(positions, chunk * rows, rows, 0)
    o, lse = attend(
        q.reshape(q.shape[0], tokens, q.shape[-1]),
        kv_new, key_value_cache, filled, positions, own_positions, 1.0 / math.sqrt(dim),
    )
    return merge(o, lse, w_out, outer, inner, dim)


def solution(mesh):
    placed = (
        P(None, "ctx"),
        P("ctx", "tp"),
        P("ctx", None, "tp"),
        P("tp", "ctx"),
        P(None, "tp", "ctx", None),
        P("ctx"),
        P(),
    )
    return jax.shard_map(
        body, mesh=mesh, in_specs=placed, out_specs=P("tp", "ctx"), check_vma=False
    )
```

time: 341 us -> 162 us (0.48)
  Pallas kernels: 0 us -> 157 us
  waiting for transfers between devices: 110 us -> 0 us
  blocking collectives: 106 us -> 0 us
  matrix products: 52.4 us -> 0 us
  other arithmetic: 26.1 us -> 0 us
  local copies, waits for them, and re-layouts: 20.9 us -> 4.87 us
  between operations: 13.6 us -> 0.73 us
  starting transfers between devices: 10.1 us -> 0 us
    pallas_call x0 -> x3, Pallas kernels: none -> 157 us  [the longest x1 55.7 us: attend(): pl.pallas_call(functools.partial(attend_kernel, scale, math.gcd(slots, 51...]
    psum x1 -> x0, blocking collectives: 106 us -> none  [body(): lax.psum(jnp.dot(hidden_input, w_in, preferred_element_type=jnp.float32),...]
    dot_general x12 -> x0, matrix products: 52.4 us -> none  [the longest x4 26.7 us: block_step(): jnp.einsum('kgrs,ksd->kgrd', probs.astype(jnp.bfloat16), val_block, prefe...]
    all_to_all x2 -> x0, waiting for transfers between devices: 44.5 us -> none  [the longest x1 43.6 us: body(): lax.all_to_all(cache_out[None], 'ctx', split_axis=1, concat_axis=0, tiled...]
    all_gather x1 -> x0, waiting for transfers between devices: 40.7 us -> none  [body(): lax.all_gather(attended, 'ctx', axis=0, tiled=True)]
    reduce_scatter x1 -> x0, waiting for transfers between devices: 24.8 us -> none  [body(): lax.psum_scatter(part_out, 'tp', scatter_dimension=0, tiled=True)]
    reduce_sum x7 -> x0, other arithmetic: 17.5 us -> none  [the longest x4 16.3 us: block_step(): denom = denom * rescale + jnp.sum(probs, axis=-1)]
    all_to_all x2 -> x0, starting transfers between devices: 10 us -> none  [the longest x1 5.55 us: body(): lax.all_to_all(cache_log[None], 'ctx', split_axis=1, concat_axis=0, tiled...]
  transfers between devices with their start and end apart: 4 -> 0, of which waited for: 4 -> 0; matrix products, arithmetic and copies ran while one was open for 2% -> 0% of each run, Pallas kernels for 0% -> 0%
where the time goes in v1:
time: 162 us
  Pallas kernels  157 us (97%)
  local copies, waits for them, and re-layouts  4.87 us (3%)
    pallas_call x1, Pallas kernels, attend(): pl.pallas_call(functools.partial(attend_kernel, scale, math.gcd(slots, 51...  55.7 us
    pallas_call x1, Pallas kernels, project(): pl.pallas_call(functools.partial(project_kernel, outer, inner, q_blocks),...  53.2 us
    pallas_call x1, Pallas kernels, merge(): pl.pallas_call(functools.partial(merge_kernel, outer, inner, tp_size, dim...  47.7 us
    unnamed x8, local copies, waits for them, and re-layouts  3.31 us

profile of v1, /device:TPU:1, one launch (start us, length us, event | category | flops | bytes accessed | tf_op | source)
XLA Modules:
  0.0 162.2 jit_solution(9054391502005037058)
XLA Ops:
  0.7 0.8 dynamic_slice.3
  1.4 0.8 copy.8.posq_ref
  2.2 0.0 copy-start
  2.2 1.6 copy.9
  3.8 0.0 copy-start.2
  3.9 1.0 copy-done.2
  4.9 53.2 %project.1 = (bf16[4,2,4,32,512]{4,3,2,1,0:T(8,128)(2,1)S(1)}, bf16[32,512]{1,0:T(8,128)(2,1)S(1)}) custom-call(bf16[2,128,1024]{2,1,0:T(8,128)(2,1)S(1)} %bitcast.12, bf16[1024,2048]{1,0:T(8,128)(2,1)} %wq_ref.1, bf16[1024,512]{1,0:T(8,128)(2,1)S(1)} %bitcast.9), custom_call_target="tpu_custom_call" | custom-call | tf_op jit(solution)/shard_map/project/pallas_call | solution.py:155
  58.1 0.0 copy-done
  58.1 0.0 copy-start.1
  58.1 55.7 %attend.1 = (bf16[4,256,512]{2,1,0:T(8,128)(2,1)S(1)}, f32[256,128]{1,0:T(8,128)S(1)}) custom-call(s32[1]{0:T(128)S(6)} %copy.11.filled_ref, bf16[4,256,512]{2,1,0:T(8,128)(2,1)S(1)} %bitcast.10, bf16[2,2,4096,128]{3,2,1,0:T(8,128)(2,1)S(1)} %copy-done, bf16[2,2,4096,128]{3,2,1,0:T(8,128)(2,1)S(1)} %copy-done, ...), custom_call_target="tpu_custom_call" | custom-call | tf_op jit(solution)/shard_map/attend/pallas_call | solution.py:259
  113.9 0.0 copy-done.1
  113.9 47.7 %merge.1 = bf16[64,1024]{1,0:T(8,128)(2,1)S(1)} custom-call(bf16[4,2,128,512]{3,2,1,0:T(8,128)(2,1)S(1)} %bitcast.11, f32[2,128,128]{2,1,0:T(8,128)S(1)} %bitcast.13, bf16[2048,1024]{1,0:T(8,128)(2,1)S(1)} %copy-done.1), custom_call_target="tpu_custom_call" | custom-call | tf_op jit(solution)/shard_map/merge/pallas_call | solution.py:433
  161.6 0.7 copy.12
  (1 shorter events, 0.0 us)
Async XLA Ops:
  2.2 55.9 %copy-start = (bf16[2,2,4096,128]{3,2,1,0:T(8,128)(2,1)S(1)}, bf16[2,2,4096,128]{3,2,1,0:T(8,128)(2,1)}, u32[]{:S(2)}) copy-start(bf16[2,2,4096,128]{3,2,1,0:T(8,128)(2,1)} %v_ref.1) | copy-start | bytes 12582916
  3.8 1.0 copy-start.2
  58.1 55.8 %copy-start.1 = (bf16[2048,1024]{1,0:T(8,128)(2,1)S(1)}, bf16[2048,1024]{1,0:T(8,128)(2,1)}, u32[]{:S(2)}) copy-start(bf16[2048,1024]{1,0:T(8,128)(2,1)} %w_ref.1) | copy-start | bytes 12582916

commit v2 on v0

v2 whole, which is shorter than its diff:
```python
import functools
import math

import jax
import jax.numpy as jnp
from jax import lax
from jax.experimental import pallas as pl
from jax.experimental.pallas import tpu as pltpu
from jax.sharding import PartitionSpec as P

MESH = pl.DeviceIdType.MESH
HIDE = -1e30
LOG2E = 1.4426950408889634


def factor(shards):
    for inner in (8, 2) if shards > 8 else (2,):
        if shards % inner == 0:
            return shards // inner, inner
    return shards, 1


def greet(peers):
    barrier = pltpu.get_barrier_semaphore()
    for peer in peers:
        pl.semaphore_signal(barrier, inc=1, device_id=peer, device_id_type=MESH)
    pl.semaphore_wait(barrier, len(peers))


def peers_of(outer, inner):
    me = lax.axis_index("ctx")
    z = me // inner
    x = me % inner
    xs = [(x + d) % inner for d in range(1, inner)]
    zs = [(z + d) % outer for d in range(1, outer)]
    x_ids = [{"ctx": z * inner + v} for v in xs]
    z_ids = [{"ctx": v * inner + x} for v in zs]
    return x, z, xs, zs, x_ids, z_ids


def remote(src, dst, sems, place, peer):
    return pltpu.make_async_remote_copy(
        src_ref=src,
        dst_ref=dst,
        send_sem=sems[0].at[place],
        recv_sem=sems[1].at[place],
        device_id=peer,
        device_id_type=MESH,
    )


NT = (((1,), (1,)), ((), ()))


def layer_kernel(
    outer, inner, tp_size, kv_heads, dim, scale, kb,
    filled_ref, hid_ref, posq_ref, posk_ref, wq_ref, wkv_ref, cache_ref, wo_ref,
    out_ref,
    w_buf, k_aug, v_raw, v_aug, wo_buf,
    part_x, recv_x, acc, recv_z, kv_new, q_buf,
    o_buf, lse, o_recv, lse_recv, mid, mid_lse, mid_recv, mid_lse_recv, weights, att,
    part, part_low, recv_t,
    w_sem, k_sem, v_sem, wo_sem,
    s1, r1, s2, r2, s3, r3, s4, r4, s5, r5, s6, r6, s7, r7, s8, r8, s9, r9, sa, ra, st, rt,
):
    cw = kv_heads * dim
    per = kv_heads
    q_blocks = q_buf.shape[0]
    blocks = q_blocks + 2
    group = q_blocks * per // kv_heads
    rows = acc.shape[2]
    half = outer * rows
    tokens = inner * half
    slots = v_raw.shape[1]
    chunk = cw // outer
    x, z, xs, zs, x_ids, z_ids = peers_of(outer, inner)
    tp = lax.axis_index("tp")
    ts = [(tp + d) % tp_size for d in range(1, tp_size)]
    t_ids = [{"tp": v} for v in ts]

    loads = [
        pltpu.make_async_copy(wkv_ref, w_buf.at[:, pl.ds(0, 2 * cw)], w_sem.at[0]),
        pltpu.make_async_copy(wq_ref, w_buf.at[:, pl.ds(2 * cw, q_blocks * cw)], w_sem.at[1]),
    ]
    k_loads = [
        pltpu.make_async_copy(cache_ref.at[0, g], k_aug.at[g, :, pl.ds(0, dim)], k_sem.at[g])
        for g in range(kv_heads)
    ]
    v_loads = [
        pltpu.make_async_copy(cache_ref.at[1, g], v_raw.at[g], v_sem.at[g])
        for g in range(kv_heads)
    ]
    wo_load = pltpu.make_async_copy(wo_ref, wo_buf, wo_sem)
    for load in loads + k_loads + v_loads + [wo_load]:
        load.start()
    greet(x_ids + z_ids + t_ids)
    for load in loads:
        load.wait()

    def x1(b):
        return [remote(part_x.at[b, d], recv_x.at[b, d], (s1, r1), (b, d), p)
                for d, p in enumerate(x_ids)]

    def z1(b):
        return [remote(acc.at[b, zs[d]], recv_z.at[b, d], (s2, r2), (b, d), p)
                for d, p in enumerate(z_ids)]

    def zg(i):
        return [remote(q_buf.at[i, x, z], q_buf.at[i, x, z], (s3, r3), (i, d), p)
                for d, p in enumerate(z_ids)]

    def xg(i):
        return [remote(q_buf.at[i, x], q_buf.at[i, x], (s4, r4), (i, d), p)
                for d, p in enumerate(x_ids)]

    def xl(i):
        return [remote(lse.at[i, xs[d]], lse_recv.at[i, d], (s5, r5), (i, d), p)
                for d, p in enumerate(x_ids)]

    def xo(i):
        return [remote(o_buf.at[i, xs[d]], o_recv.at[i, d], (s6, r6), (i, d), p)
                for d, p in enumerate(x_ids)]

    def zl(i):
        return [remote(mid_lse.at[i], mid_lse_recv.at[i, d], (s7, r7), (i, d), p)
                for d, p in enumerate(z_ids)]

    def zo(i):
        return [remote(mid.at[i, zs[d]], mid_recv.at[i, d], (s8, r8), (i, d), p)
                for d, p in enumerate(z_ids)]

    def za(i):
        return [remote(att.at[x, i, z], att.at[x, i, z], (s9, r9), (i, d), p)
                for d, p in enumerate(z_ids)]

    def xa(i):
        return [remote(att.at[x, i], att.at[x, i], (sa, ra), (i, d), p)
                for d, p in enumerate(x_ids)]

    def start(copies):
        for copy in copies:
            copy.start()

    def arrive(copies):
        for copy in copies:
            copy.wait_recv()

    def ship(b):
        w = w_buf[:, pl.ds(pl.multiple_of(b * cw, cw), cw)]
        for d in range(inner - 1):
            part_x[b, d] = jnp.dot(hid_ref[xs[d]], w, preferred_element_type=jnp.float32)
        start(x1(b))
        own = jnp.dot(hid_ref[x], w, preferred_element_type=jnp.float32)
        acc[b] = own.reshape(outer, rows, cw)

    def add_x(b):
        arrive(x1(b))
        total = acc[b]
        for d in range(inner - 1):
            total += recv_x[b, d].reshape(outer, rows, cw)
        acc[b] = total
        start(z1(b))

    def add_z(b):
        arrive(z1(b))
        total = acc[b, z]
        for d in range(outer - 1):
            total += recv_z[b, d]
        low = total.astype(jnp.bfloat16)

        @pl.when(b < 2)
        def _():
            kv_new[b] = low

        @pl.when(b >= 2)
        def _():
            q_buf[b - 2, x, z] = low
            start(zg(b - 2))

    def spread(i):
        arrive(zg(i))
        start(xg(i))

    def attend(i):
        arrive(xg(i))
        g = i * per // group
        c = scale * LOG2E
        lane = lax.broadcasted_iota(jnp.int32, (tokens, dim), 1)
        one = jnp.where(lane == 0, 1.0, 0.0).astype(jnp.bfloat16)
        q = q_buf[i].reshape(tokens, cw)
        qs = [q[:, j * dim : (j + 1) * dim] for j in range(per)]
        aug = [jnp.concatenate([v, one], axis=1) for v in qs]
        k_fresh = kv_new[0, :, pl.ds(pl.multiple_of(g * dim, dim), dim)]
        v_fresh = kv_new[1, :, pl.ds(pl.multiple_of(g * dim, dim), dim)]
        v_fresh = v_fresh.astype(jnp.float32).T
        v_fresh = jnp.concatenate(
            [v_fresh, jnp.ones((16, rows), jnp.float32)], axis=0
        ).astype(jnp.bfloat16)
        seen = posk_ref[...] <= posq_ref[...]

        def scores(j, b):
            if b < 0:
                return jnp.where(seen, lax.dot_general(
                    k_fresh, qs[j], NT, preferred_element_type=jnp.float32), HIDE)
            return lax.dot_general(
                k_aug[g, b * kb : (b + 1) * kb, :], aug[j], NT, preferred_element_type=jnp.float32
            )

        order = [(j, b) for b in list(range(slots // kb)) + [-1] for j in range(per)]
        state = [None] * per
        coming = scores(*order[0])
        for n, (j, b) in enumerate(order):
            s = coming
            if n + 1 < len(order):
                coming = scores(*order[n + 1])
            high = jnp.max(s, axis=0, keepdims=True)
            if state[j] is not None:
                high = jnp.maximum(state[j][0], high)
            p = jnp.exp2((s - high) * c).astype(jnp.bfloat16)
            v = v_fresh if b < 0 else v_aug[g, :, b * kb : (b + 1) * kb]
            t = jnp.dot(v, p, preferred_element_type=jnp.float32)
            if state[j] is not None:
                t = t + state[j][1] * jnp.exp2((state[j][0] - high) * c)
            state[j] = (high, t)
        for j in range(per):
            high, t = state[j]
            denom = t[dim : dim + 1, :]
            value = (t[:dim] / denom).astype(jnp.bfloat16)
            log = high * scale + jnp.log(denom)
            for v in range(inner):
                o_buf[i, v, j * dim : (j + 1) * dim, :] = value[:, v * half : (v + 1) * half]
                lse[i, v, j : j + 1, :] = log[:, v * half : (v + 1) * half]
        start(xl(i))
        start(xo(i))

    def shares(logs):
        top = functools.reduce(jnp.maximum, logs)
        parts = [jnp.exp(v - top) for v in logs]
        total = sum(parts[1:], parts[0])
        return [w / total for w in parts], top + jnp.log(total)

    def blend_x(i):
        arrive(xl(i))
        ws, log = shares([lse[i, x]] + [lse_recv[i, d] for d in range(inner - 1)])
        mid_lse[i] = log
        start(zl(i))
        arrive(xo(i))
        pieces = []
        for j in range(per):
            span = slice(j * dim, (j + 1) * dim)
            total = ws[0][j : j + 1] * o_buf[i, x, span, :].astype(jnp.float32)
            for d in range(inner - 1):
                total += ws[d + 1][j : j + 1] * o_recv[i, d, span, :].astype(jnp.float32)
            pieces.append(total.reshape(dim // chunk, chunk, half).astype(jnp.bfloat16))
        for j in range(per):
            n = dim // chunk
            mid[i, j * n : (j + 1) * n] = pieces[j]
        start(zo(i))

    def blend_z(i):
        arrive(zl(i))
        ws, _ = shares([mid_lse[i]] + [mid_lse_recv[i, d] for d in range(outer - 1)])
        for d in range(outer):
            weights[d] = ws[d]
        head = z * chunk // dim
        arrive(zo(i))
        total = weights[0, pl.ds(head, 1), :] * mid[i, z].astype(jnp.float32)
        for d in range(outer - 1):
            total += weights[d + 1, pl.ds(head, 1), :] * mid_recv[i, d].astype(jnp.float32)
        att[x, i, z] = total.astype(jnp.bfloat16)
        start(za(i))

    def spread_att(i):
        arrive(za(i))
        start(xa(i))

    ahead = 2
    for b in range(ahead):
        ship(b)
    lse[...] = jnp.zeros_like(lse)
    filled = filled_ref[0]
    row = lax.broadcasted_iota(jnp.int32, (slots, dim), 0)
    col = lax.broadcasted_iota(jnp.int32, (slots, dim), 1)
    bias = jnp.where((row >= filled) & (col == 0), HIDE, 0.0).astype(jnp.bfloat16)
    for g in range(kv_heads):
        k_aug[g, :, dim:] = bias
        v_aug[g, dim:, :] = jnp.ones((16, slots), jnp.bfloat16)
        v_loads[g].wait()
        v_aug[g, :dim, :] = v_raw[g].T
        k_loads[g].wait()

    def step(t, carry):
        def stage(lag, first, last, run):
            i = t - lag

            @pl.when((i >= first) & (i < last))
            def _():
                run(i)

        stage(-ahead, ahead, blocks, ship)
        stage(0, 0, blocks, add_x)
        stage(1, 0, blocks, add_z)
        stage(4, 0, q_blocks, spread)
        stage(5, 0, q_blocks, attend)
        stage(6, 0, q_blocks, blend_x)
        stage(7, 0, q_blocks, blend_z)
        stage(8, 0, q_blocks, spread_att)
        return carry

    lax.fori_loop(0, q_blocks + 8, step, 0)

    wo_load.wait()
    for d, v in enumerate([x] + xs):
        if d > 0:
            for i in range(q_blocks):
                xa(i)[inner - 1 - d].wait_recv()
        lhs = att[v].reshape(q_blocks * cw, half).T
        part[v] = jnp.dot(lhs, wo_buf[...], preferred_element_type=jnp.float32)
    share = out_ref.shape[0]
    whole = part[...].reshape(tp_size, share, part.shape[2])
    part_low[...] = whole.astype(jnp.bfloat16)
    last = [remote(part_low.at[ts[d]], recv_t.at[d], (st, rt), d, p) for d, p in enumerate(t_ids)]
    start(last)
    own = part.reshape(tp_size, share, part.shape[2])[tp]
    for d, copy in enumerate(last):
        copy.wait_recv()
        own += recv_t[d].astype(jnp.float32)
    out_ref[...] = own.astype(out_ref.dtype)
    for copy in last:
        copy.wait_send()

    def drain(kinds):
        def run(i, carry):
            for kind in kinds:
                for copy in kind(i):
                    copy.wait_send()
            return carry
        return run

    lax.fori_loop(0, blocks, drain([x1, z1]), 0)
    lax.fori_loop(0, q_blocks, drain([zg, xg, xl, xo, zl, zo, za, xa]), 0)


def body(hidden_input, w_query, key_value_weight, w_out, key_value_cache, filled, positions):
    tokens, width = hidden_input.shape
    shards = lax.axis_size("ctx")
    tp_size = lax.axis_size("tp")
    outer, inner = factor(shards)
    rows = tokens // shards
    half = outer * rows
    _, kv_heads, slots, dim = key_value_cache.shape
    cw = kv_heads * dim
    q_blocks = w_query.shape[1] // cw
    blocks = q_blocks + 2
    chunk = cw // outer
    out_width = w_out.shape[1]
    share = tokens // tp_size
    me = lax.axis_index("ctx")
    owned = (me % inner) * outer + me // inner
    own_positions = lax.dynamic_slice_in_dim(positions, owned * rows, rows, 0)
    nx, nz, nt = max(inner - 1, 1), max(outer - 1, 1), max(tp_size - 1, 1)
    dma = pltpu.SemaphoreType.DMA
    vmem = pl.BlockSpec(memory_space=pltpu.VMEM)
    hbm = pl.BlockSpec(memory_space=pl.ANY)
    low, full = jnp.bfloat16, jnp.float32
    pairs = []
    for count, peers in (
        (blocks, nx), (blocks, nz), (q_blocks, nz), (q_blocks, nx), (q_blocks, nx),
        (q_blocks, nx), (q_blocks, nz), (q_blocks, nz), (q_blocks, nz), (q_blocks, nx),
    ):
        pairs += [dma((count, peers)), dma((count, peers))]
    return pl.pallas_call(
        functools.partial(
            layer_kernel, outer, inner, tp_size, kv_heads, dim, 1.0 / math.sqrt(dim),
            math.gcd(slots, 1024),
        ),
        out_shape=jax.ShapeDtypeStruct((share, out_width), low),
        in_specs=[pl.BlockSpec(memory_space=pltpu.SMEM), vmem, vmem, vmem, hbm, hbm, hbm, hbm],
        out_specs=vmem,
        scratch_shapes=[
            pltpu.VMEM((width, blocks * cw), low),
            pltpu.VMEM((kv_heads, slots, 2 * dim), low),
            pltpu.VMEM((kv_heads, slots, dim), low),
            pltpu.VMEM((kv_heads, dim + 16, slots), low),
            pltpu.VMEM(w_out.shape, low),
            pltpu.VMEM((blocks, nx, half, cw), full),
            pltpu.VMEM((blocks, nx, half, cw), full),
            pltpu.VMEM((blocks, outer, rows, cw), full),
            pltpu.VMEM((blocks, nz, rows, cw), full),
            pltpu.VMEM((2, rows, cw), low),
            pltpu.VMEM((q_blocks, inner, outer, rows, cw), low),
            pltpu.VMEM((q_blocks, inner, cw, half), low),
            pltpu.VMEM((q_blocks, inner, 8, half), full),
            pltpu.VMEM((q_blocks, nx, cw, half), low),
            pltpu.VMEM((q_blocks, nx, 8, half), full),
            pltpu.VMEM((q_blocks, outer, chunk, half), low),
            pltpu.VMEM((q_blocks, 8, half), full),
            pltpu.VMEM((q_blocks, nz, chunk, half), low),
            pltpu.VMEM((q_blocks, nz, 8, half), full),
            pltpu.VMEM((outer, 8, half), full),
            pltpu.VMEM((inner, q_blocks, outer, chunk, half), low),
            pltpu.VMEM((inner, half, out_width), full),
            pltpu.VMEM((tp_size, share, out_width), low),
            pltpu.VMEM((nt, share, out_width), low),
            dma((2,)), dma((kv_heads,)), dma((kv_heads,)), dma(()),
            *pairs,
            dma((nt,)), dma((nt,)),
        ],
        compiler_params=pltpu.CompilerParams(
            collective_id=0, has_side_effects=True, vmem_limit_bytes=60 << 20
        ),
        name="layer",
    )(
        filled, hidden_input.reshape(inner, half, width), positions.reshape(1, tokens),
        own_positions.reshape(rows, 1), w_query, key_value_weight.reshape(width, -1),
        key_value_cache, w_out,
    )


def solution(mesh):
    placed = (
        P(None, "ctx"),
        P("ctx", "tp"),
        P("ctx", None, "tp"),
        P("tp", "ctx"),
        P(None, "tp", "ctx", None),
        P("ctx"),
        P(),
    )
    return jax.shard_map(
        body, mesh=mesh, in_specs=placed, out_specs=P("tp", "ctx"), check_vma=False
    )
```

time: 341 us -> 109 us (0.32)
  waiting for transfers between devices: 110 us -> 0 us
  blocking collectives: 106 us -> 0 us
  Pallas kernels: 0 us -> 103 us
  matrix products: 52.4 us -> 0 us
  other arithmetic: 26.1 us -> 0 us
  local copies, waits for them, and re-layouts: 20.9 us -> 5.46 us
  between operations: 13.6 us -> 0.66 us
  starting transfers between devices: 10.1 us -> 0 us
    psum x1 -> x0, blocking collectives: 106 us -> none  [body(): lax.psum(jnp.dot(hidden_input, w_in, preferred_element_type=jnp.float32),...]
    pallas_call x0 -> x1, Pallas kernels: none -> 103 us  [body(): pl.pallas_call(functools.partial(layer_kernel, outer, inner, tp_size, kv_...]
    dot_general x12 -> x0, matrix products: 52.4 us -> none  [the longest x4 26.7 us: block_step(): jnp.einsum('kgrs,ksd->kgrd', probs.astype(jnp.bfloat16), val_block, prefe...]
    all_to_all x2 -> x0, waiting for transfers between devices: 44.5 us -> none  [the longest x1 43.6 us: body(): lax.all_to_all(cache_out[None], 'ctx', split_axis=1, concat_axis=0, tiled...]
    all_gather x1 -> x0, waiting for transfers between devices: 40.7 us -> none  [body(): lax.all_gather(attended, 'ctx', axis=0, tiled=True)]
    reduce_scatter x1 -> x0, waiting for transfers between devices: 24.8 us -> none  [body(): lax.psum_scatter(part_out, 'tp', scatter_dimension=0, tiled=True)]
    reduce_sum x7 -> x0, other arithmetic: 17.5 us -> none  [the longest x4 16.3 us: block_step(): denom = denom * rescale + jnp.sum(probs, axis=-1)]
    all_to_all x2 -> x0, starting transfers between devices: 10 us -> none  [the longest x1 5.55 us: body(): lax.all_to_all(cache_log[None], 'ctx', split_axis=1, concat_axis=0, tiled...]
  transfers between devices with their start and end apart: 4 -> 0, of which waited for: 4 -> 0; matrix products, arithmetic and copies ran while one was open for 2% -> 0% of each run, Pallas kernels for 0% -> 0%
where the time goes in v2:
time: 109 us
  Pallas kernels  103 us (94%)
  local copies, waits for them, and re-layouts  5.46 us (5%)
    pallas_call x1, Pallas kernels, body(): pl.pallas_call(functools.partial(layer_kernel, outer, inner, tp_size, kv_...  103 us
    unnamed x2, local copies, waits for them, and re-layouts  4.01 us

profile of v2, /device:TPU:1, one launch (start us, length us, event | category | flops | bytes accessed | tf_op | source)
XLA Modules:
  0.0 108.9 jit_solution(10958255226957900653)
XLA Ops:
  0.7 0.8 dynamic-slice_bitcast_fusion
  1.4 0.7 copy.8.posk_ref
  2.1 2.4 %copy.9 = bf16[128,8,2,256]{3,1,2,0:T(8,128)(2,1)} copy(bf16[128,8,2,256]{3,2,1,0:T(2,128)(2,1)} %bitcast.7) | data formatting | bytes 2097152
  4.5 102.8 %layer.1 = bf16[64,1024]{1,0:T(8,128)(2,1)} custom-call(s32[1]{0:T(128)S(6)} %copy.11.filled_ref, bf16[2,128,1024]{2,1,0:T(8,128)(2,1)} %bitcast.8, s32[1,256]{1,0:T(1,128)} %bitcast.9, s32[32,1]{1,0:T(8,128)} %copy.8.posk_ref, bf16[1024,2048]{1,0:T(8,128)(2,1)} %wq_ref.1, bf16[1024,512]{1,0:T(8,128)(2,1)} %bitcast.6, bf16[2,2,4096,128]{3,2,1,0:T(8,128)(2,1)} %cache_ref.1, ...), custom_call_target="tpu_custom_call" | custom-call | tf_op jit(solution)/shard_map/layer/pallas_call | solution.py:372
  107.3 1.6 %copy.12 = bf16[64,1024]{1,0:T(8,128)(2,1)} copy(bf16[64,1024]{1,0:T(8,128)(2,1)} %layer.1) | data formatting | bytes 262144

commit v3 on v2

--- a/solution.py
+++ b/solution.py
@@ -54,12 +54,12 @@
 
 def layer_kernel(
     outer, inner, tp_size, kv_heads, dim, scale, kb,
-    filled_ref, hid_ref, posq_ref, posk_ref, wq_ref, wkv_ref, cache_ref, wo_ref,
+    filled_ref, hid_ref, posq_ref, wq_ref, wkv_ref, cache_ref, wo_ref,
     out_ref,
     w_buf, k_aug, v_raw, v_aug, wo_buf,
     part_x, recv_x, acc, recv_z, kv_new, q_buf,
     o_buf, lse, o_recv, lse_recv, mid, mid_lse, mid_recv, mid_lse_recv, weights, att,
-    part, part_low, recv_t,
+    part, part_low, recv_t, places,
     w_sem, k_sem, v_sem, wo_sem,
     s1, r1, s2, r2, s3, r3, s4, r4, s5, r5, s6, r6, s7, r7, s8, r8, s9, r9, sa, ra, st, rt,
 ):
@@ -196,7 +196,7 @@
         v_fresh = jnp.concatenate(
             [v_fresh, jnp.ones((16, rows), jnp.float32)], axis=0
         ).astype(jnp.bfloat16)
-        seen = posk_ref[...] <= posq_ref[...]
+        seen = places[pl.ds((x * outer + z) * rows, rows), 0:1] <= posq_ref[...]
 
         def scores(j, b):
             if b < 0:
@@ -274,10 +274,25 @@
         arrive(za(i))
         start(xa(i))
 
-    ahead = 2
+    def product(i, v):
+        lhs = att[v, i].reshape(cw, half).T
+        w = wo_buf[pl.ds(pl.multiple_of(i * cw, cw), cw), :]
+        part[v] += jnp.dot(lhs, w, preferred_element_type=jnp.float32)
+
+    def project_own(i):
+        product(i, x)
+
+    def project_rest(i):
+        arrive(xa(i))
+        for v in xs:
+            product(i, v)
+
+    ahead = 3
     for b in range(ahead):
         ship(b)
     lse[...] = jnp.zeros_like(lse)
+    part[...] = jnp.zeros_like(part)
+    places[...] = jnp.broadcast_to(posq_ref[...], (128, tokens)).T
     filled = filled_ref[0]
     row = lax.broadcasted_iota(jnp.int32, (slots, dim), 0)
     col = lax.broadcasted_iota(jnp.int32, (slots, dim), 1)
@@ -288,6 +303,7 @@
         v_loads[g].wait()
         v_aug[g, :dim, :] = v_raw[g].T
         k_loads[g].wait()
+    wo_load.wait()
 
     def step(t, carry):
         def stage(lag, first, last, run):
@@ -305,17 +321,12 @@
         stage(6, 0, q_blocks, blend_x)
         stage(7, 0, q_blocks, blend_z)
         stage(8, 0, q_blocks, spread_att)
+        stage(8, 0, q_blocks, project_own)
+        stage(9, 0, q_blocks, project_rest)
         return carry
 
-    lax.fori_loop(0, q_blocks + 8, step, 0)
-
-    wo_load.wait()
-    for d, v in enumerate([x] + xs):
-        if d > 0:
-            for i in range(q_blocks):
-                xa(i)[inner - 1 - d].wait_recv()
-        lhs = att[v].reshape(q_blocks * cw, half).T
-        part[v] = jnp.dot(lhs, wo_buf[...], preferred_element_type=jnp.float32)
+    lax.fori_loop(0, q_blocks + 9, step, 0)
+
     share = out_ref.shape[0]
     whole = part[...].reshape(tp_size, share, part.shape[2])
     part_low[...] = whole.astype(jnp.bfloat16)
@@ -355,9 +366,6 @@
     chunk = cw // outer
     out_width = w_out.shape[1]
     share = tokens // tp_size
-    me = lax.axis_index("ctx")
-    owned = (me % inner) * outer + me // inner
-    own_positions = lax.dynamic_slice_in_dim(positions, owned * rows, rows, 0)
     nx, nz, nt = max(inner - 1, 1), max(outer - 1, 1), max(tp_size - 1, 1)
     dma = pltpu.SemaphoreType.DMA
     vmem = pl.BlockSpec(memory_space=pltpu.VMEM)
@@ -375,7 +383,7 @@
             math.gcd(slots, 1024),
         ),
         out_shape=jax.ShapeDtypeStruct((share, out_width), low),
-        in_specs=[pl.BlockSpec(memory_space=pltpu.SMEM), vmem, vmem, vmem, hbm, hbm, hbm, hbm],
+        in_specs=[pl.BlockSpec(memory_space=pltpu.SMEM), vmem, vmem, hbm, hbm, hbm, hbm],
         out_specs=vmem,
         scratch_shapes=[
             pltpu.VMEM((width, blocks * cw), low),
@@ -402,6 +410,7 @@
             pltpu.VMEM((inner, half, out_width), full),
             pltpu.VMEM((tp_size, share, out_width), low),
             pltpu.VMEM((nt, share, out_width), low),
+            pltpu.VMEM((tokens, 128), jnp.int32),
             dma((2,)), dma((kv_heads,)), dma((kv_heads,)), dma(()),
             *pairs,
             dma((nt,)), dma((nt,)),
@@ -412,7 +421,7 @@
         name="layer",
     )(
         filled, hidden_input.reshape(inner, half, width), positions.reshape(1, tokens),
-        own_positions.reshape(rows, 1), w_query, key_value_weight.reshape(width, -1),
+        w_query, key_value_weight.reshape(width, -1),
         key_value_cache, w_out,
     )
 

time: 109 us -> 107 us (0.982)
  local copies, waits for them, and re-layouts: 5.46 us -> 4.01 us
    reshape x2 -> x0, local copies, waits for them, and re-layouts: 1.45 us -> none  [body(): own_positions.reshape(rows, 1)]
where the time goes in v3:
time: 107 us
  Pallas kernels  102 us (95%)
  local copies, waits for them, and re-layouts  4.01 us (4%)
    pallas_call x1, Pallas kernels, body(): pl.pallas_call(functools.partial(layer_kernel, outer, inner, tp_size, kv_...  102 us
    unnamed x2, local copies, waits for them, and re-layouts  4.01 us

profile of v3, /device:TPU:1, one launch (start us, length us, event | category | flops | bytes accessed | tf_op | source)
XLA Modules:
  0.0 106.6 jit_solution(12216325857788698339)
XLA Ops:
  0.7 2.4 %copy.8 = bf16[128,8,2,256]{3,1,2,0:T(8,128)(2,1)} copy(bf16[128,8,2,256]{3,2,1,0:T(2,128)(2,1)} %bitcast.5) | data formatting | bytes 2097152
  3.1 101.9 %layer.1 = bf16[64,1024]{1,0:T(8,128)(2,1)} custom-call(s32[1]{0:T(128)S(6)} %copy.10.filled_ref, bf16[2,128,1024]{2,1,0:T(8,128)(2,1)} %bitcast.6, s32[1,256]{1,0:T(1,128)} %bitcast.7, bf16[1024,2048]{1,0:T(8,128)(2,1)} %wq_ref.1, bf16[1024,512]{1,0:T(8,128)(2,1)} %bitcast.4, bf16[2,2,4096,128]{3,2,1,0:T(8,128)(2,1)} %cache_ref.1, bf16[2048,1024]{1,0:T(8,128)(2,1)} %wo_ref.1), custom_call_target="tpu_custom_call" | custom-call | tf_op jit(solution)/shard_map/layer/pallas_call | solution.py:380
  105.0 1.6 %copy.11 = bf16[64,1024]{1,0:T(8,128)(2,1)} copy(bf16[64,1024]{1,0:T(8,128)(2,1)} %layer.1) | data formatting | bytes 262144
